TPU v7x, 256 devices: a whole 4x4x8 slice. The times are simulated.
256 devices in a mesh: section: 2 (over y_lo), dp: 4 (over y_hi, core), shard: 32 (over x, z).
Axes of the slice: x: 4, y: 4 (y_hi: 2, y_lo: 2; y = y_hi * 2 + y_lo), z: 8, core: 2. Of those that a mesh axis runs over, the one named last changes fastest.
Arguments:
- norm_input: bfloat16 [2, 4, 4096, 3584], P('section', 'dp', 'shard'), may hold values from -6 to 6
- norm_gain: float32 [2, 3584], P('section'), may hold values from 0.1 to 1.9
- branch_grad: bfloat16 [2, 4, 4096, 3584], P('section', 'dp', 'shard'), may hold values from -6 to 6
- residual_grad: bfloat16 [2, 4, 4096, 3584], P('section', 'dp', 'shard'), may hold values from -6 to 6
- down_weight: bfloat16 [2, 14336, 3584], P('section', 'shard'), may hold values from -0.09375 to 0.09375
Outputs:
- boundary_grad: bfloat16 [2, 4, 4096, 3584], P('section', 'dp', 'shard')
- gain_grad: float32 [2, 3584], P('section')
- unit_grads: bfloat16 [2, 4, 4096, 14336], P('section', 'dp', None, 'shard')
All inputs are finite; a program needn't handle non-finite values.
Results may differ from a plain program's by a relative error of at most 0.0049.
Values may be sent and summed in bfloat16 or wider, within the bound.
A program may use at most 128 MiB of HBM per device.

v0:
```python
import jax
import jax.numpy as jnp
from jax import lax
from jax.sharding import Mesh
from jax.sharding import PartitionSpec as P

DP_SHARD = ("dp_0", "dp_1", "shard_0", "shard_1")
SHARD = ("shard_0", "shard_1")
DP = ("dp_0", "dp_1")
epsilon = 1e-05


def one_axis_at_a_time(array, axes):
    for axis in axes:
        array = lax.psum(array, axis)
    return array


def from_partner(block, axis, distance):
    count = lax.axis_size(axis)
    route = []
    for low in range(count):
        high = low | 1 << distance
        if high != low and high < count:
            route += [(low, high), (high, low)]
    return lax.ppermute(block, axis, route)


def norm_backward(inputs, gain_row, branch, residual):
    values = inputs.astype(jnp.float32)
    inverse = lax.rsqrt(jnp.mean(values * values, axis=-1, keepdims=True) + epsilon)
    normed = values * inverse
    upstream = branch.astype(jnp.float32)
    scaled = upstream * gain_row
    project = jnp.mean(scaled * normed, axis=-1, keepdims=True)
    boundary = (residual.astype(jnp.float32) + inverse * (scaled - normed * project)).astype(
        jnp.bfloat16
    )
    return (boundary, jnp.sum(upstream * normed, axis=0))


def per_device(norm_input, norm_gain, branch_grad, residual_grad, down_weight):
    weight = down_weight[0]
    boundary, gain_part = norm_backward(
        norm_input[0, 0], norm_gain[0], branch_grad[0, 0], residual_grad[0, 0]
    )
    gain_total = one_axis_at_a_time(gain_part, DP_SHARD)
    arrived = from_partner(boundary, "section", 0)
    fresh = jnp.einsum(
        "nd,hd->nh",
        lax.all_gather(arrived, SHARD, axis=0, tiled=True),
        weight,
        preferred_element_type=jnp.float32,
    ).astype(jnp.bfloat16)
    gain_grad = gain_total / fresh.shape[0]
    return (boundary[None, None], gain_grad[None], fresh[None, None])


def solution(mesh):
    split = Mesh(
        mesh.devices.reshape(mesh.shape["section"], 2, 2, 4, 8),
        ("section", "dp_0", "dp_1", "shard_0", "shard_1"),
    )
    return jax.shard_map(
        per_device,
        mesh=split,
        in_specs=(
            P("section", DP, SHARD, None),
            P("section", None),
            P("section", DP, SHARD, None),
            P("section", DP, SHARD, None),
            P("section", SHARD, None),
        ),
        out_specs=(
            P("section", DP, SHARD, None),
            P("section", None),
            P("section", DP, None, SHARD),
        ),
        check_vma=False,
    )
```

profile of v0, /device:TPU:1, one launch (start us, length us, event | category | flops | bytes accessed | tf_op | source)
XLA Modules:
  0.0 275.5 jit_solution(16686822337064339081)
XLA Ops:
  7.2 0.0 copy-start
  7.2 0.0 all-gather.2.cloned.1.call-start
  7.2 1.6 fusion.17
  8.8 0.8 reduce
  9.6 0.0 copy-start.1
  9.6 0.0 copy-start.2
  9.6 2.3 fusion.16
  11.9 0.0 copy-done.1
  11.9 0.0 copy-done.2
  11.9 1.8 fusion.11
  13.8 2.2 collective-permute-start
  16.0 18.8 %collective-permute-done = bf16[128,3584]{1,0:T(8,128)(2,1)} collective-permute-done((bf16[128,3584]{1,0:T(8,128)(2,1)S(1)}, bf16[128,3584]{1,0:T(8,128)(2,1)}, u32[]{:S(2)}, u32[]{:S(2)}) %collective-permute-start) | collective-permute-done | bytes 917536 | tf_op jit(solution)/shard_map/ppermute | solution.py:26
  34.8 0.0 all-gather.2.cloned.1.call-update
  34.8 10.5 %psum.28 = f32[3584]{0:T(1024)S(1)} all-reduce(f32[3584]{0:T(1024)S(1)} %get-tuple-element.3), channel_id=1, replica_groups=mesh['section'=2,'dp_0'=2,'dp_1'=2,'shard_0'=4,'shard_1'=8] {'dp_0'}, use_global_device_ids=true, to_apply=%region_3.0 | all-reduce | flops 3584 | bytes 28672 | tf_op jit(solution)/shard_map/psum | solution.py:15
  45.4 6.7 %psum.29 = f32[3584]{0:T(1024)S(1)} all-reduce(f32[3584]{0:T(1024)S(1)} %psum.28), channel_id=1, replica_groups=mesh['section'=2,'dp_0'=2,'dp_1'=2,'shard_0'=4,'shard_1'=8] {'dp_1'}, use_global_device_ids=true, to_apply=%region_4.0 | all-reduce | flops 3584 | bytes 28672 | tf_op jit(solution)/shard_map/psum | solution.py:15
  52.1 14.8 %psum.30 = f32[3584]{0:T(1024)S(1)} all-reduce(f32[3584]{0:T(1024)S(1)} %psum.29), channel_id=1, replica_groups=mesh['section'=2,'dp_0'=2,'dp_1'=2,'shard_0'=4,'shard_1'=8] {'shard_0'}, use_global_device_ids=true, to_apply=%region_5.0 | all-reduce | flops 3584 | bytes 28672 | tf_op jit(solution)/shard_map/psum | solution.py:15
  67.0 28.4 %psum.31 = f32[3584]{0:T(1024)S(1)} all-reduce(f32[3584]{0:T(1024)S(1)} %psum.30), channel_id=1, replica_groups=mesh['section'=2,'dp_0'=2,'dp_1'=2,'shard_0'=4,'shard_1'=8] {'shard_1'}, use_global_device_ids=true, to_apply=%region_6.0 | all-reduce | flops 3584 | bytes 28672 | tf_op jit(solution)/shard_map/psum | solution.py:15
  95.4 0.6 broadcast_in_dim.4
  96.0 3.3 %fusion.12 = bf16[1,1,128,3584]{3,2,1,0:T(8,128)(2,1)} fusion(bf16[1,1,128,3584]{3,2,1,0:T(8,128)(2,1)} %param.8, bf16[1,1,128,3584]{3,2,1,0:T(8,128)(2,1)} %param.7, bf16[1,1,128,3584]{3,2,1,0:T(8,128)(2,1)} %param.5, f32[128]{0:T(128)S(1)} %broadcast_multiply_fusion.1, f32[3584]{0:T(1024)S(1)} %reduce, f32[128]{0:T(128)S(1)} %add_rsqrt_fusion), kind=kLoop, calls=%fused_computation.19 | loop fusion | flops 4587520 | bytes 3685376 | tf_op jit(solution)/shard_map/convert_element_type | solution.py:36
  99.3 149.4 %all-gather.2.cloned.1.call-done = bf16[4096,3584]{1,0:T(8,128)(2,1)} async-done(((bf16[128,3584]{1,0:T(8,128)(2,1)}), bf16[4096,3584]{1,0:T(8,128)(2,1)}) %all-gather.2.cloned.1.call-update) | async-done | bytes 29360144 | tf_op jit(solution)/shard_map/all_gather | solution.py:51
  248.7 0.0 copy-done
  248.7 20.0 %fusion = bf16[1,1,4096,448]{2,3,1,0:T(8,128)(2,1)} fusion(bf16[4096,3584]{1,0:T(8,128)(2,1)} %all-gather.2.cloned.1.call-done, bf16[1,448,3584]{2,1,0:T(8,128)(2,1)S(1)} %copy-done), kind=kOutput, calls=%fused_computation.1 | convolution fusion | flops 13155172352 | bytes 36241408 | tf_op jit(solution)/shard_map/nd,hd->nh/dot_general | solution.py:49
  (3 shorter events, 0.0 us)
Async XLA Ops:
  7.2 241.5 %copy-start = (bf16[1,448,3584]{2,1,0:T(8,128)(2,1)S(1)}, bf16[1,448,3584]{2,1,0:T(8,128)(2,1)}, u32[]{:S(2)}) copy-start(bf16[1,448,3584]{2,1,0:T(8,128)(2,1)} %param.9) | copy-start | bytes 9633796
  7.2 241.5 %all-gather.2.cloned.1.call-start = ((), (), s32[]{:S(2)}) async-start(), calls=%async_computation | async-start | bytes 30277632 | tf_op jit(solution)/shard_map/all_gather | solution.py:51
  9.6 2.3 copy-start.1
  9.6 2.3 copy-start.2
  13.8 21.0 %collective-permute-start = (bf16[128,3584]{1,0:T(8,128)(2,1)S(1)}, bf16[128,3584]{1,0:T(8,128)(2,1)}, u32[]{:S(2)}, u32[]{:S(2)}) collective-permute-start(bf16[128,3584]{1,0:T(8,128)(2,1)S(1)} %fusion.11), channel_id=1, source_target_pairs={{0,128},{128,0},{1,129},{129,1},{2,130},{130,2},{3,131},{131,3},{4... | collective-permute-start | bytes 2752520 | tf_op jit(solution)/shard_map/ppermute | solution.py:26
Sparse Core Ops, SparseCore 0:
  35.0 213.6 all-gather.1
where the time goes:
time: 276 us
  waiting for transfers between devices  168 us (61%)
  blocking collectives  60.5 us (22%)
  matrix products  20 us (7%)
  between operations  14.1 us (5%)
  other arithmetic  9.79 us (4%)
    all_gather x1, waiting for transfers between devices, per_device(): lax.all_gather(arrived, SHARD, axis=0, tiled=True)  149 us
    psum x4, blocking collectives, one_axis_at_a_time(): array = lax.psum(array, axis)  60.5 us
    dot_general x1, matrix products, per_device(): jnp.einsum('nd,hd->nh', lax.all_gather(arrived, SHARD, axis=0, tiled=True...  20 us
    ppermute x1, waiting for transfers between devices, from_partner(): return lax.ppermute(block, axis, route)  18.8 us
  transfers between devices with their start and end apart: 2, of which 2 were waited for; matrix products, arithmetic and copies ran while one was open for 1% of the time, Pallas kernels for 0%

commit v1 on v0

--- a/solution.py
+++ b/solution.py
@@ -48,7 +48,9 @@
     arrived = from_partner(boundary, "section", 0)
     fresh = jnp.einsum(
         "nd,hd->nh",
-        lax.all_gather(arrived, SHARD, axis=0, tiled=True),
+        jnp.concatenate(
+            lax.all_to_all(jnp.stack([arrived] * lax.axis_size(SHARD)), SHARD, 0, 0), axis=0
+        ),
         weight,
         preferred_element_type=jnp.float32,
     ).astype(jnp.bfloat16)

time: 276 us -> 802 us (2.91)
  the two profiles are of different devices: /device:TPU:1 before, /device:TPU:28 now
where the time goes in v1:
time: 802 us; the launch traced here: 801 us
  blocking collectives  726 us (91%)
  waiting for transfers between devices  21.3 us (3%)
  matrix products  20 us (2%)
  starting transfers between devices  12.5 us (2%)
  local copies, waits for them, and re-layouts  10.6 us (1%)
  other arithmetic  9.78 us (1%)
    psum x4, blocking collectives, one_axis_at_a_time(): array = lax.psum(array, axis)  726 us
    ppermute x1, waiting for transfers between devices, from_partner(): return lax.ppermute(block, axis, route)  21.3 us
    dot_general x1, matrix products, per_device(): jnp.einsum('nd,hd->nh', jnp.concatenate(lax.all_to_all(jnp.stack([arrived...  20 us
  transfers between devices with their start and end apart: 2, of which 1 were waited for; matrix products, arithmetic and copies ran while one was open for 0% of the time, Pallas kernels for 0%

profile of v1, /device:TPU:28, one launch (start us, length us, event | category | flops | bytes accessed | tf_op | source)
XLA Modules:
  0.0 801.3 jit_solution(7774146186817901470)
XLA Ops:
  0.6 0.0 copy-start
  0.6 1.6 fusion.17
  2.3 0.8 reduce
  3.0 0.0 copy-start.1
  3.0 0.0 copy-start.2
  3.0 2.3 fusion.16
  5.3 0.0 copy-done.1
  5.4 0.0 copy-done.2
  5.4 1.8 fusion.11
  7.2 0.8 collective-permute-start
  8.0 21.3 %collective-permute-done = bf16[128,3584]{1,0:T(8,128)(2,1)S(1)} collective-permute-done((bf16[128,3584]{1,0:T(8,128)(2,1)S(1)}, bf16[128,3584]{1,0:T(8,128)(2,1)S(1)}, u32[]{:S(2)}, u32[]{:S(2)}) %collective-permute-start) | collective-permute-done | bytes 917536 | tf_op jit(solution)/shard_map/ppermute | solution.py:26
  29.4 9.9 %stack.2 = bf16[32,128,3584]{2,1,0:T(8,128)(2,1)} broadcast(bf16[128,3584]{1,0:T(8,128)(2,1)S(1)} %collective-permute-done), dimensions={1,2} | broadcast | bytes 30277632 | tf_op jit(solution)/shard_map/stack | solution.py:52
  39.3 11.6 %all-to-all-start = ((bf16[32,128,3584]{2,1,0:T(8,128)(2,1)}), bf16[32,128,3584]{2,1,0:T(8,128)(2,1)}, u32[]{:S(2)}, u32[]{:S(2)}) async-start(bf16[32,128,3584]{2,1,0:T(8,128)(2,1)} %stack.2), calls=%async_computation | async-start | bytes 58720256 | tf_op jit(solution)/shard_map/all_to_all | solution.py:52
  50.9 9.4 %psum.28 = f32[3584]{0:T(1024)S(1)} all-reduce(f32[3584]{0:T(1024)S(1)} %get-tuple-element.3), channel_id=1, replica_groups=mesh['section'=2,'dp_0'=2,'dp_1'=2,'shard_0'=4,'shard_1'=8] {'dp_0'}, use_global_device_ids=true, to_apply=%region_3.0 | all-reduce | flops 3584 | bytes 28672 | tf_op jit(solution)/shard_map/psum | solution.py:15
  60.3 3.3 psum.29
  63.7 53.8 %psum.30 = f32[3584]{0:T(1024)S(1)} all-reduce(f32[3584]{0:T(1024)S(1)} %psum.29), channel_id=1, replica_groups=mesh['section'=2,'dp_0'=2,'dp_1'=2,'shard_0'=4,'shard_1'=8] {'shard_0'}, use_global_device_ids=true, to_apply=%region_5.0 | all-reduce | flops 3584 | bytes 28672 | tf_op jit(solution)/shard_map/psum | solution.py:15
  117.5 659.8 %psum.31 = f32[3584]{0:T(1024)S(1)} all-reduce(f32[3584]{0:T(1024)S(1)} %psum.30), channel_id=1, replica_groups=mesh['section'=2,'dp_0'=2,'dp_1'=2,'shard_0'=4,'shard_1'=8] {'shard_1'}, use_global_device_ids=true, to_apply=%region_6.0 | all-reduce | flops 3584 | bytes 28672 | tf_op jit(solution)/shard_map/psum | solution.py:15
  777.3 0.6 broadcast_in_dim.4
  777.9 3.3 fusion.12
  781.2 0.0 all-to-all-done
  781.2 0.0 copy-done
  781.2 20.0 %fusion = bf16[1,1,4096,448]{2,3,1,0:T(8,128)(2,1)} fusion(bf16[4096,3584]{1,0:T(8,128)(2,1)} %bitcast.3, bf16[1,448,3584]{2,1,0:T(8,128)(2,1)S(1)} %copy-done), kind=kOutput, calls=%fused_computation.1 | convolution fusion | flops 13155172352 | bytes 36241408 | tf_op jit(solution)/shard_map/nd,hd->nh/dot_general | solution.py:49
  (3 shorter events, 0.0 us)
Async XLA Ops:
  0.6 780.6 %copy-start = (bf16[1,448,3584]{2,1,0:T(8,128)(2,1)S(1)}, bf16[1,448,3584]{2,1,0:T(8,128)(2,1)}, u32[]{:S(2)}) copy-start(bf16[1,448,3584]{2,1,0:T(8,128)(2,1)} %param.9) | copy-start | bytes 9633796
  3.0 2.3 copy-start.1
  3.0 2.3 copy-start.2
  7.2 22.2 %collective-permute-start = (bf16[128,3584]{1,0:T(8,128)(2,1)S(1)}, bf16[128,3584]{1,0:T(8,128)(2,1)S(1)}, u32[]{:S(2)}, u32[]{:S(2)}) collective-permute-start(bf16[128,3584]{1,0:T(8,128)(2,1)S(1)} %fusion.11), channel_id=1, source_target_pairs={{0,128},{128,0},{1,129},{129,1},{2,130},{130,2},{3,131},{131,3},{4... | collective-permute-start | bytes 2752520 | tf_op jit(solution)/shard_map/ppermute | solution.py:26
  39.3 741.9 %all-to-all-start = ((bf16[32,128,3584]{2,1,0:T(8,128)(2,1)}), bf16[32,128,3584]{2,1,0:T(8,128)(2,1)}, u32[]{:S(2)}, u32[]{:S(2)}) async-start(bf16[32,128,3584]{2,1,0:T(8,128)(2,1)} %stack.2), calls=%async_computation | async-start | bytes 58720256 | tf_op jit(solution)/shard_map/all_to_all | solution.py:52
